TPU v7x, 32 devices: a whole 2x2x4 slice. The times are simulated.
32 devices in a mesh: outer: 4 (over y, x), inner: 8 (over z, core).
Axes of the slice: x: 2, y: 2, z: 4, core: 2. Of those that a mesh axis runs over, the one named last changes fastest.
Arguments:
- p_factor: bfloat16 [56, 56, 16384], P('outer', None, 'inner'), may hold values from -24 to 24
- q_factor: bfloat16 [56, 56, 16384], P(None, None, 'inner'), may hold values from -6 to 6
- truncation: bfloat16 [3136, 56], P('outer'), may hold values from -0.109375 to 0.109375
Outputs:
- gram: float32 [3136, 3136], P('outer', 'inner')
- coarse: float32 [56, 16384], P(None, 'inner')
All inputs are finite; a program needn't handle non-finite values.
Results may differ from a plain program's by a relative error of at most 0.003.
Values may be sent and summed in bfloat16 or wider, within the bound.
No kernel may reach another device: no remote copies, remote signals or barrier semaphores. Data moves between devices by JAX's collectives and lax.ppermute only.
A program may use at most 128 MiB of HBM per device.

v0:
```python
import math
import jax
import jax.numpy as jnp
from jax import lax
from jax.sharding import PartitionSpec as P


def contract(factor, q_factor):
    bond_size = q_factor.shape[0]
    paired = jnp.einsum("imc,jmc->ijc", factor, q_factor, preferred_element_type=jnp.float32)
    paired = paired / math.sqrt(q_factor.shape[1])
    return paired.reshape(factor.shape[0] * bond_size, factor.shape[2]).astype(jnp.bfloat16)


def body(p_factor, q_factor, truncation):
    columns = p_factor.shape[2]
    own_rows = contract(p_factor, q_factor)
    gathered = lax.all_gather(own_rows, "outer", axis=0, tiled=True)
    partial_value = lax.dot_general(
        own_rows, gathered, (((1,), (1,)), ((), ())), preferred_element_type=jnp.float32
    )
    total_columns = columns * lax.axis_size("inner")
    gram = lax.psum_scatter(partial_value, "inner", scatter_dimension=1, tiled=True) / total_columns
    local_term = lax.dot_general(
        truncation, own_rows, (((0,), (0,)), ((), ())), preferred_element_type=jnp.float32
    )
    absorbed = lax.psum(local_term, "outer")
    squares = lax.psum(jnp.sum(absorbed * absorbed), "inner")
    norm_scale = jnp.sqrt(squares / (absorbed.shape[0] * total_columns) + 1e-06)
    return (gram, absorbed / norm_scale)


def solution(mesh):
    return jax.shard_map(
        body,
        mesh=mesh,
        in_specs=(P("outer", None, "inner"), P(None, None, "inner"), P("outer", None)),
        out_specs=(P("outer", "inner"), P(None, "inner")),
        check_vma=False,
    )
```

profile of v0, /device:TPU:0, one launch (start us, length us, event | category | flops | bytes accessed | tf_op | source)
XLA Modules:
  0.0 385.2 jit_solution(4690721399324301520)
XLA Ops:
  7.2 0.0 copy-start
  7.2 0.0 all-gather.2.cloned.1.call-start
  7.2 10.5 %copy.11 = bf16[14,56,2048]{1,0,2:T(8,128)(2,1)} copy(bf16[14,56,2048]{2,1,0:T(8,128)(2,1)} %param.3) | data formatting | bytes 6422528 | tf_op args[0]
  17.7 31.2 %copy.10 = bf16[56,56,2048]{1,0,2:T(8,128)(2,1)} copy(bf16[56,56,2048]{2,1,0:T(8,128)(2,1)} %param.4) | data formatting | bytes 25690112 | tf_op args[1]
  48.9 22.2 %fusion = bf16[14,56,2048]{1,0,2:T(8,128)(2,1)} fusion(bf16[56,56,2048]{1,0,2:T(8,128)(2,1)} %copy.10, bf16[14,56,2048]{1,0,2:T(8,128)(2,1)} %copy.11), kind=kOutput, calls=%fused_computation.1 | convolution fusion | flops 183042048 | bytes 19267584 | tf_op jit(solution)/shard_map/imc,jmc->ijc/dot_general | solution.py:10
  71.1 9.8 %copy.12 = bf16[14,56,2048]{2,1,0:T(8,128)(2,1)} copy(bf16[14,56,2048]{1,0,2:T(8,128)(2,1)} %fusion) | data formatting | bytes 6422528 | tf_op jit(solution)/shard_map/convert_element_type | solution.py:12
  80.9 0.0 copy-start.2
  80.9 0.0 all-gather.2.cloned.1.call-update
  80.9 0.0 all-reduce.3.cloned.1.call-start
  81.0 0.0 copy-done
  81.0 3.6 convolution_bitcast_fusion
  84.6 0.0 all-reduce.3.cloned.1.call-update
  84.6 0.0 reduce-scatter.4.cloned.1.call-start
  84.6 123.9 %all-gather.2.cloned.1.call-done = bf16[3136,2048]{1,0:T(8,128)(2,1)} async-done(((bf16[784,2048]{1,0:T(8,128)(2,1)}), bf16[3136,2048]{1,0:T(8,128)(2,1)}) %all-gather.2.cloned.1.call-update) | async-done | bytes 12845072 | tf_op jit(solution)/shard_map/all_gather | solution.py:18
  208.5 0.0 copy-done.2
  208.5 0.0 copy-start.1
  208.5 18.2 %fusion.1 = f32[784,3136]{0,1:T(8,128)} fusion(bf16[784,2048]{1,0:T(8,128)(2,1)S(1)} %bitcast.14, bf16[3136,2048]{1,0:T(8,128)(2,1)} %all-gather.2.cloned.1.call-done), kind=kOutput, calls=%fused_computation.6 | convolution fusion | flops 10070523904 | bytes 25890816 | tf_op jit(solution)/shard_map/dot_general | solution.py:19
  226.7 0.0 reduce-scatter.4.cloned.1.call-update
  226.8 30.0 %all-reduce.3.cloned.1.call-done = f32[56,2048]{1,0:T(8,128)} async-done(((f32[56,2048]{1,0:T(8,128)}), f32[56,2048]{1,0:T(8,128)}) %all-reduce.3.cloned.1.call-update) | async-done | bytes 458768 | tf_op jit(solution)/shard_map/psum | solution.py:27
  256.8 1.7 multiply_reduce_fusion
  258.5 16.8 %psum.15 = f32[]{:T(128)} all-reduce(f32[]{:T(128)} %multiply_reduce_fusion), channel_id=1, replica_groups=mesh['outer'=4,'inner'=8] {'inner'}, use_global_device_ids=true, to_apply=%region_3.0 | all-reduce | flops 1 | bytes 8 | tf_op jit(solution)/shard_map/psum | solution.py:28
  276.0 1.8 broadcast_divide_fusion
  277.8 98.4 %reduce-scatter.4.cloned.1.call-done = f32[784,392]{0,1:T(8,128)} async-done(((f32[784,3136]{0,1:T(8,128)}), f32[784,392]{0,1:T(8,128)}) %reduce-scatter.4.cloned.1.call-update) | async-done | bytes 1229328
  376.2 2.5 broadcast_multiply_fusion
  378.7 0.0 copy-done.1
Async XLA Ops:
  7.2 73.8 %copy-start = (bf16[784,56]{0,1:T(8,128)(2,1)S(1)}, bf16[784,56]{0,1:T(8,128)(2,1)}, u32[]{:S(2)}) copy-start(bf16[784,56]{0,1:T(8,128)(2,1)} %param.5) | copy-start | bytes 263428
  7.2 201.3 %all-gather.2.cloned.1.call-start = ((), (), s32[]{:S(2)}) async-start(), calls=%async_computation.1 | async-start | bytes 16056320 | tf_op jit(solution)/shard_map/all_gather | solution.py:18
  80.9 127.6 %copy-start.2 = (bf16[14,56,2048]{2,1,0:T(8,128)(2,1)S(1)}, bf16[14,56,2048]{2,1,0:T(8,128)(2,1)}, u32[]{:S(2)}) copy-start(bf16[14,56,2048]{2,1,0:T(8,128)(2,1)} %copy.12) | copy-start | bytes 9633796
  80.9 175.8 %all-reduce.3.cloned.1.call-start = ((), (), s32[]{:S(2)}) async-start(), calls=%async_computation.2 | async-start | bytes 917504 | tf_op jit(solution)/shard_map/psum | solution.py:27
  84.6 291.6 %reduce-scatter.4.cloned.1.call-start = ((), (), s32[]{:S(2)}) async-start(), calls=%async_computation.3 | async-start | bytes 12644352
  208.5 170.2 %copy-start.1 = (bf16[784,56]{0,1:T(8,128)(2,1)S(1)}, bf16[784,56]{0,1:T(8,128)(2,1)}, u32[]{:S(2)}) copy-start(bf16[784,56]{0,1:T(8,128)(2,1)} %param.5) | copy-start | bytes 263428
Sparse Core Ops, SparseCore 0:
  81.1 127.3 all-gather.1
  212.1 44.6 all-reduce.2
  259.2 116.9 reduce-scatter.3
where the time goes:
time: 387 us; the launch traced here: 385 us
  waiting for transfers between devices  252 us (65%)
  local copies, waits for them, and re-layouts  51.5 us (13%)
  matrix products  44 us (11%)
  blocking collectives  16.8 us (4%)
  between operations  14.5 us (4%)
  other arithmetic  6.09 us (2%)
    all_gather x1, waiting for transfers between devices, body(): gathered = lax.all_gather(own_rows, 'outer', axis=0, tiled=True)  124 us
    unnamed x4, waiting for transfers between devices  98.4 us
    unnamed x8, local copies, waits for them, and re-layouts  41.7 us
    psum x1, waiting for transfers between devices, body(): absorbed = lax.psum(local_term, 'outer')  30 us
    dot_general x1, matrix products, contract(): jnp.einsum('imc,jmc->ijc', factor, q_factor, preferred_element_type=jnp.f...  22.2 us
    dot_general x1, matrix products, body(): lax.dot_general(own_rows, gathered, (((1,), (1,)), ((), ())), preferred_e...  18.2 us
    psum x1, blocking collectives, body(): squares = lax.psum(jnp.sum(absorbed * absorbed), 'inner')  16.8 us
    convert_element_type x1, local copies, waits for them, and re-layouts, contract(): paired.reshape(factor.shape[0] * bond_size, factor.shape[2])  9.78 us
  transfers between devices with their start and end apart: 3, of which 3 were waited for; matrix products, arithmetic and copies ran while one was open for 7% of the time, Pallas kernels for 0%

commit v1 on v0

--- a/solution.py
+++ b/solution.py
@@ -24,7 +24,8 @@
     local_term = lax.dot_general(
         truncation, own_rows, (((0,), (0,)), ((), ())), preferred_element_type=jnp.float32
     )
-    absorbed = lax.psum(local_term, "outer")
+    parts = lax.all_gather(local_term, "outer")
+    absorbed = jnp.sum(parts, axis=0)
     squares = lax.psum(jnp.sum(absorbed * absorbed), "inner")
     norm_scale = jnp.sqrt(squares / (absorbed.shape[0] * total_columns) + 1e-06)
     return (gram, absorbed / norm_scale)

time: 387 us -> 374 us (0.966)
  waiting for transfers between devices: 252 us -> 239 us
    psum x1 -> x0, waiting for transfers between devices: 30 us -> none  [body(): absorbed = lax.psum(local_term, 'outer')]
    all_gather x0 -> x1, waiting for transfers between devices: none -> 17.3 us  [body(): parts = lax.all_gather(local_term, 'outer')]
where the time goes in v1:
time: 374 us; the launch traced here: 372 us
  waiting for transfers between devices  239 us (64%)
  local copies, waits for them, and re-layouts  51.5 us (14%)
  matrix products  44 us (12%)
  blocking collectives  17.2 us (5%)
  between operations  14.5 us (4%)
  other arithmetic  5.71 us (2%)
    all_gather x1, waiting for transfers between devices, body(): gathered = lax.all_gather(own_rows, 'outer', axis=0, tiled=True)  124 us
    unnamed x4, waiting for transfers between devices  98.3 us
    unnamed x8, local copies, waits for them, and re-layouts  41.7 us
    dot_general x1, matrix products, contract(): jnp.einsum('imc,jmc->ijc', factor, q_factor, preferred_element_type=jnp.f...  22.2 us
    dot_general x1, matrix products, body(): lax.dot_general(own_rows, gathered, (((1,), (1,)), ((), ())), preferred_e...  18.2 us
    all_gather x1, waiting for transfers between devices, body(): parts = lax.all_gather(local_term, 'outer')  17.3 us
    psum x1, blocking collectives, body(): squares = lax.psum(jnp.sum(absorbed * absorbed), 'inner')  17.2 us
    convert_element_type x1, local copies, waits for them, and re-layouts, contract(): paired.reshape(factor.shape[0] * bond_size, factor.shape[2])  9.78 us
  transfers between devices with their start and end apart: 3, of which 3 were waited for; matrix products, arithmetic and copies ran while one was open for 7% of the time, Pallas kernels for 0%

profile of v1, /device:TPU:0, one launch (start us, length us, event | category | flops | bytes accessed | tf_op | source)
XLA Modules:
  0.0 372.5 jit_solution(10731519565874705026)
XLA Ops:
  7.2 0.0 copy-start
  7.2 0.0 all-gather.4.cloned.1.call-start
  7.2 10.5 %copy.11 = bf16[14,56,2048]{1,0,2:T(8,128)(2,1)} copy(bf16[14,56,2048]{2,1,0:T(8,128)(2,1)} %param.3) | data formatting | bytes 6422528 | tf_op args[0]
  17.7 31.2 %copy.10 = bf16[56,56,2048]{1,0,2:T(8,128)(2,1)} copy(bf16[56,56,2048]{2,1,0:T(8,128)(2,1)} %param.4) | data formatting | bytes 25690112 | tf_op args[1]
  48.9 22.2 %fusion = bf16[14,56,2048]{1,0,2:T(8,128)(2,1)} fusion(bf16[56,56,2048]{1,0,2:T(8,128)(2,1)} %copy.10, bf16[14,56,2048]{1,0,2:T(8,128)(2,1)} %copy.11), kind=kOutput, calls=%fused_computation.1 | convolution fusion | flops 183042048 | bytes 19267584 | tf_op jit(solution)/shard_map/imc,jmc->ijc/dot_general | solution.py:10
  71.1 9.8 %copy.12 = bf16[14,56,2048]{2,1,0:T(8,128)(2,1)} copy(bf16[14,56,2048]{1,0,2:T(8,128)(2,1)} %fusion) | data formatting | bytes 6422528 | tf_op jit(solution)/shard_map/convert_element_type | solution.py:12
  80.9 0.0 copy-start.2
  80.9 0.0 all-gather.4.cloned.1.call-update
  80.9 0.0 all-gather.6.cloned.1.call-start
  81.0 0.0 copy-done
  81.0 3.6 convolution_bitcast_fusion
  84.6 0.0 all-gather.6.cloned.1.call-update
  84.6 0.0 reduce-scatter.4.cloned.1.call-start
  84.6 123.8 %all-gather.4.cloned.1.call-done = bf16[3136,2048]{1,0:T(8,128)(2,1)} async-done(((bf16[784,2048]{1,0:T(8,128)(2,1)}), bf16[3136,2048]{1,0:T(8,128)(2,1)}) %all-gather.4.cloned.1.call-update) | async-done | bytes 12845072 | tf_op jit(solution)/shard_map/all_gather | solution.py:18
  208.5 0.0 copy-done.2
  208.5 18.2 %fusion.1 = f32[784,3136]{0,1:T(8,128)} fusion(bf16[784,2048]{1,0:T(8,128)(2,1)S(1)} %bitcast.15, bf16[3136,2048]{1,0:T(8,128)(2,1)} %all-gather.4.cloned.1.call-done), kind=kOutput, calls=%fused_computation.6 | convolution fusion | flops 10070523904 | bytes 25890816 | tf_op jit(solution)/shard_map/dot_general | solution.py:19
  226.7 0.0 copy-start.1
  226.7 0.0 reduce-scatter.4.cloned.1.call-update
  226.7 17.3 %all-gather.6.cloned.1.call-done = f32[224,2048]{1,0:T(8,128)} async-done(((f32[56,2048]{1,0:T(8,128)}), f32[224,2048]{1,0:T(8,128)}) %all-gather.6.cloned.1.call-update) | async-done | bytes 1835024 | tf_op jit(solution)/shard_map/all_gather | solution.py:27
  244.1 1.7 reduce_sum.18
  245.8 0.7 multiply_reduce_fusion
  246.5 17.2 %psum.7 = f32[]{:T(128)} all-reduce(f32[]{:T(128)} %multiply_reduce_fusion), channel_id=1, replica_groups=mesh['outer'=4,'inner'=8] {'inner'}, use_global_device_ids=true, to_apply=%region_3.0 | all-reduce | flops 1 | bytes 8 | tf_op jit(solution)/shard_map/psum | solution.py:29
  264.3 0.8 broadcast_divide_fusion
  265.2 98.3 %reduce-scatter.4.cloned.1.call-done = f32[784,392]{0,1:T(8,128)} async-done(((f32[784,3136]{0,1:T(8,128)}), f32[784,392]{0,1:T(8,128)}) %reduce-scatter.4.cloned.1.call-update) | async-done | bytes 1229328
  363.4 2.5 broadcast_multiply_fusion
  365.9 0.0 copy-done.1
Async XLA Ops:
  7.2 73.8 %copy-start = (bf16[784,56]{0,1:T(8,128)(2,1)S(1)}, bf16[784,56]{0,1:T(8,128)(2,1)}, u32[]{:S(2)}) copy-start(bf16[784,56]{0,1:T(8,128)(2,1)} %param.5) | copy-start | bytes 263428
  7.2 201.3 %all-gather.4.cloned.1.call-start = ((), (), s32[]{:S(2)}) async-start(), calls=%async_computation.1 | async-start | bytes 16056320 | tf_op jit(solution)/shard_map/all_gather | solution.py:18
  80.9 127.6 %copy-start.2 = (bf16[14,56,2048]{2,1,0:T(8,128)(2,1)S(1)}, bf16[14,56,2048]{2,1,0:T(8,128)(2,1)}, u32[]{:S(2)}) copy-start(bf16[14,56,2048]{2,1,0:T(8,128)(2,1)} %copy.12) | copy-start | bytes 9633796
  80.9 163.1 %all-gather.6.cloned.1.call-start = ((), (), s32[]{:S(2)}) async-start(), calls=%async_computation.2 | async-start | bytes 2293760 | tf_op jit(solution)/shard_map/all_gather | solution.py:27
  84.6 278.8 %reduce-scatter.4.cloned.1.call-start = ((), (), s32[]{:S(2)}) async-start(), calls=%async_computation.3 | async-start | bytes 12644352
  226.7 139.2 %copy-start.1 = (bf16[784,56]{0,1:T(8,128)(2,1)S(1)}, bf16[784,56]{0,1:T(8,128)(2,1)}, u32[]{:S(2)}) copy-start(bf16[784,56]{0,1:T(8,128)(2,1)} %param.5) | copy-start | bytes 263428
Sparse Core Ops, SparseCore 0:
  81.1 127.3 all-gather.3
  210.9 33.1 all-gather.5
  246.4 116.9 reduce-scatter.3
